TPU v7x, 32 devices: a whole 2x2x4 slice. The times are simulated.
32 devices in a mesh: row: 4 (over y, x), col: 8 (over z, core).
Axes of the slice: x: 2, y: 2, z: 4, core: 2. Of those that a mesh axis runs over, the one named last changes fastest.
Arguments:
- teacher: bfloat16 [16384, 256], replicated, may hold values from -4 to 4
- panel_ids: int32 [2048], P('col'), may hold values from 0 to 16383
- rest_ids: int32 [4, 8, 128], P('row', 'col'), may hold values from 0 to 16383
- inverse: bfloat16 [2048, 2048], replicated, may hold values from -1 to 1, as said below
Outputs:
- trailing: float32 [8, 4, 128, 4, 8, 128], P(None, 'row', None, None, 'col')
- panel_rows: bfloat16 [4, 8, 128, 2048], P('row', 'col')
Inputs may be any that keep to these rules, and one draw needn't show every extreme that they name: `inverse`: zero above the diagonal.
All inputs are finite; a program needn't handle non-finite values.
Results may differ from a plain program's by a relative error of at most 0.0049.
Values may be sent and summed in bfloat16 or wider, within the bound.
A program may use at most 128 MiB of HBM per device.

v0:
```python
import functools

import jax
import jax.numpy as jnp
from jax import lax
from jax.experimental import pallas as pl
from jax.experimental.pallas import tpu as pltpu
from jax.sharding import PartitionSpec as P

MESH = pl.DeviceIdType.MESH


def exchange_kernel(
    n_row, n_col, rest_ref, panel_ref, table_hbm, emb_ref,
    panel_out, row_out, col_out, panel_ids, row_ids, col_ids, landed, table, picked,
    send_sem, row_sem, col_sem, panel_sem, table_sem, ids_sem,
):
    pieces = table_sem.shape[0]
    lanes = table.shape[1]
    halves = table_hbm.shape[1] // lanes
    piece = table_hbm.shape[0] // pieces

    def load(at):
        rows = pl.ds(at * piece, piece)
        return pltpu.make_async_copy(table_hbm.at[rows], landed.at[rows], table_sem.at[at])

    for at in range(pieces):
        load(at).start()
    row_at = lax.axis_index("row")
    col_at = lax.axis_index("col")
    me = row_at * n_col + col_at
    barrier = pltpu.get_barrier_semaphore()
    count = n_row * n_col

    def greet(step, carry):
        other = lax.rem(me + step, count)
        pl.semaphore_signal(
            barrier, inc=1, device_id=(other // n_col, lax.rem(other, n_col)), device_id_type=MESH
        )
        return carry

    lax.fori_loop(1, count, greet, 0)
    panel_out[col_at] = panel_ref[0]
    col_out[row_at] = rest_ref[0]
    row_role = lax.rem(me, n_row)
    place = me // n_row

    @pl.when(row_role == row_at)
    def _():
        row_out[place] = rest_ref[0]

    pl.semaphore_wait(barrier, count - 1)

    def panel_copy(slot, target):
        return pltpu.make_async_remote_copy(
            src_ref=panel_ref.at[0], dst_ref=panel_out.at[slot],
            send_sem=send_sem.at[target], recv_sem=panel_sem.at[slot],
            device_id=(row_at, target), device_id_type=MESH,
        )

    def row_copy(slot, target):
        return pltpu.make_async_remote_copy(
            src_ref=rest_ref.at[0], dst_ref=row_out.at[slot],
            send_sem=send_sem.at[n_col + target], recv_sem=row_sem.at[slot],
            device_id=(row_role, target), device_id_type=MESH,
        )

    def col_copy(slot, target):
        return pltpu.make_async_remote_copy(
            src_ref=rest_ref.at[0], dst_ref=col_out.at[slot],
            send_sem=send_sem.at[2 * n_col + target], recv_sem=col_sem.at[slot],
            device_id=(target, col_at), device_id_type=MESH,
        )

    def each(length, skip, act):
        for at in range(length):
            pl.when(jnp.logical_not(skip(at)))(functools.partial(act, at))

    to_self = lambda at: jnp.logical_and(row_role == row_at, at == col_at)
    from_self = lambda at: at * n_row + row_at == me
    each(n_col, lambda at: at == col_at, lambda at: panel_copy(col_at, at).start())
    each(n_col, to_self, lambda at: row_copy(place, at).start())
    each(n_row, lambda at: at == row_at, lambda at: col_copy(row_at, at).start())
    for at in range(pieces):
        load(at).wait()

        def widen(step, carry, at=at):
            rows = pl.ds(pl.multiple_of(at * piece + step * 64, 64), 64)
            wide = landed[rows, :].astype(jnp.float32)
            for half in range(halves):
                place = pl.ds((at * piece + step * 64) * halves + half, 64, stride=halves)
                table[place, :] = wide[:, half * lanes : (half + 1) * lanes]
            return carry

        lax.fori_loop(0, piece // 64, widen, 0)
    each(n_col, lambda at: at == col_at, lambda at: panel_copy(at, at).wait_recv())
    each(n_col, from_self, lambda at: row_copy(at, at).wait_recv())
    each(n_row, lambda at: at == row_at, lambda at: col_copy(at, at).wait_recv())
    each(n_col, lambda at: at == col_at, lambda at: panel_copy(col_at, at).wait_send())
    each(n_col, to_self, lambda at: row_copy(place, at).wait_send())
    each(n_row, lambda at: at == row_at, lambda at: col_copy(row_at, at).wait_send())
    groups = ((panel_out, panel_ids), (row_out, row_ids), (col_out, col_ids))
    moves = [pltpu.make_async_copy(src, dst, ids_sem.at[at]) for at, (src, dst) in enumerate(groups)]
    for move in moves:
        move.start()
    for move in moves:
        move.wait()
    first = 0
    for _, ids in groups:
        count, _, span = ids.shape

        def pick(block, carry, ids=ids, span=span, first=first):
            start = pl.multiple_of((first + block * span) * halves, span * halves)
            home = picked.at[pl.ds(start, span * halves)]
            for lane in range(span):
                row = ids[block, 0, lane] * halves
                home[lane * halves : (lane + 1) * halves, :] = table[pl.ds(row, halves), :]
            return carry

        lax.fori_loop(0, count, pick, 0)
        first += count * span

    def narrow(step, carry):
        rows = pl.ds(pl.multiple_of(step * 64, 64), 64)
        for half in range(halves):
            value = picked[pl.ds(step * 64 * halves + half, 64, stride=halves), :]
            emb_ref[rows, half * lanes : (half + 1) * lanes] = value.astype(jnp.bfloat16)
        return carry

    lax.fori_loop(0, first // 64, narrow, 0)


def exchange(rest_ids, panel_ids, teacher, n_row, n_col):
    stretch = rest_ids.shape[2]
    width = panel_ids.shape[0]
    total = n_col * width + (n_col + n_row) * stretch
    shapes = ((n_col, 1, width), (n_col, 1, stretch), (n_row, 1, stretch))
    vmem = pl.BlockSpec(memory_space=pltpu.VMEM)
    return pl.pallas_call(
        functools.partial(exchange_kernel, n_row, n_col),
        out_shape=jax.ShapeDtypeStruct((total, teacher.shape[1]), teacher.dtype),
        in_specs=[vmem, vmem, pl.BlockSpec(memory_space=pltpu.HBM)],
        out_specs=vmem,
        scratch_shapes=[pltpu.VMEM(shape, jnp.int32) for shape in shapes]
        + [pltpu.SMEM(shape, jnp.int32) for shape in shapes]
        + [
            pltpu.VMEM(teacher.shape, teacher.dtype),
            pltpu.VMEM((teacher.size // 128, 128), jnp.float32),
            pltpu.VMEM((total * teacher.shape[1] // 128, 128), jnp.float32),
            pltpu.SemaphoreType.DMA((2 * n_col + n_row,)),
            pltpu.SemaphoreType.DMA((n_col,)),
            pltpu.SemaphoreType.DMA((n_row,)),
            pltpu.SemaphoreType.DMA((n_col,)),
            pltpu.SemaphoreType.DMA((8,)),
            pltpu.SemaphoreType.DMA((3,)),
        ],
        compiler_params=pltpu.CompilerParams(
            collective_id=0, has_side_effects=True, vmem_limit_bytes=52 * 1024 * 1024
        ),
        name="exchange",
    )(rest_ids, panel_ids.reshape(1, 1, width), teacher)


def nt_dot(left, right):
    return lax.dot_general(left, right, (((1,), (1,)), ((), ())), preferred_element_type=jnp.float32)


def gram_kernel(n_row, n_col, stretch, emb_ref, inv_hbm, trail_ref, own_ref, inv_ref, cross_ref, fac_ref, norm_ref, inv_sem):
    width = inv_hbm.shape[0]
    block = 256
    blocks = width // block
    total = emb_ref.shape[0] - width
    n_rows = n_col * stretch
    unit = 2.0 / emb_ref.shape[1] * 1.4426950408889634
    row_at = lax.axis_index("row")
    col_at = lax.axis_index("col")

    def load(at):
        rows, cols = pl.ds(at * block, block), pl.ds(0, (at + 1) * block)
        return pltpu.make_async_copy(inv_hbm.at[rows, cols], inv_ref.at[rows, cols], inv_sem.at[at])

    for at in range(blocks):
        load(at).start()

    def across(value):
        square = jnp.square(value.astype(jnp.float32))
        high = square.astype(jnp.bfloat16)
        low = (square - high.astype(jnp.float32)).astype(jnp.bfloat16)
        ones = jnp.ones((8, value.shape[1]), jnp.bfloat16)
        return (nt_dot(ones, high) + nt_dot(ones, low)) * unit

    def down(value):
        return jnp.sum(jnp.square(value.astype(jnp.float32)), axis=-1, keepdims=True) * unit

    for at in range(blocks):
        norm_ref[:, at * block : (at + 1) * block] = across(emb_ref[at * block : (at + 1) * block, :])

    def gram(left, left_norm, right, right_norm):
        return jnp.exp2(nt_dot(left, right) * (2.0 * unit) - (left_norm + right_norm))

    tile = 512

    def factor_tile(start, first):
        rows = pl.ds(start, tile)
        left = emb_ref[pl.ds(width + start, tile), :]
        left_norm = down(left)
        for at in range(blocks):
            cols = slice(at * block, (at + 1) * block)
            cross_ref[:, cols] = gram(left, left_norm, emb_ref[cols, :], norm_ref[0:1, cols]).astype(jnp.bfloat16)
            if first:
                load(at).wait()
            fac_ref[rows, cols] = nt_dot(
                cross_ref[:, : (at + 1) * block], inv_ref[cols, : (at + 1) * block]
            ).astype(jnp.bfloat16)

    factor_tile(n_rows, True)
    for start in range(n_rows + tile, total, tile):
        factor_tile(start, False)
    own_ref[...] = fac_ref[pl.ds(pl.multiple_of(n_rows + row_at * stretch, stretch), stretch), :]

    ahead = lax.broadcasted_iota(jnp.int32, (stretch, stretch), 0) - lax.broadcasted_iota(
        jnp.int32, (stretch, stretch), 1
    )
    pair = 2 if n_row % 2 == 0 else 1
    for start in range(0, n_rows, tile):
        factor_tile(start, False)
        left = emb_ref[pl.ds(width + start, tile), :]
        left_norm = down(left)
        last = (start + tile) // stretch - 1
        for low in range(0, n_row, pair):
            if last * n_row + n_row - 1 >= low * n_col:
                first_col = n_rows + low * stretch
                span = pl.ds(first_col, pair * stretch)
                right = emb_ref[pl.ds(width + first_col, pair * stretch), :]
                value = gram(left, left_norm, right, across(right)[0:1]) - nt_dot(
                    fac_ref[pl.ds(start, tile), :], fac_ref[span, :]
                )
            else:
                value = None
            for q in range(start // stretch, last + 1):
                for p in range(low, low + pair):
                    place = pl.ds(q * stretch * n_row + p, stretch, stride=n_row)
                    if q * n_row + n_row - 1 < p * n_col:
                        trail_ref[place, :] = jnp.zeros((stretch, stretch), jnp.float32)
                    else:
                        top = q * stretch - start
                        side = (p - low) * stretch
                        part = value[top : top + stretch, side : side + stretch]
                        gap = (p * n_col + col_at - q * n_row - row_at) * stretch
                        trail_ref[place, :] = jnp.where(ahead >= gap, part, 0.0)


def shards(teacher, panel_ids, rest_ids, inverse):
    n_row = lax.axis_size("row")
    n_col = lax.axis_size("col")
    stretch = rest_ids.shape[2]
    width = inverse.shape[0]
    emb = exchange(rest_ids, panel_ids, teacher, n_row, n_col)
    total = emb.shape[0] - width
    vmem = pl.BlockSpec(memory_space=pltpu.VMEM)
    trailing, own_factor = pl.pallas_call(
        functools.partial(gram_kernel, n_row, n_col, stretch),
        out_shape=(
            jax.ShapeDtypeStruct((n_col * stretch * n_row, stretch), jnp.float32),
            jax.ShapeDtypeStruct((stretch, width), jnp.bfloat16),
        ),
        in_specs=[vmem, pl.BlockSpec(memory_space=pltpu.HBM)],
        out_specs=(vmem, vmem),
        scratch_shapes=[
            pltpu.VMEM((width, width), jnp.bfloat16),
            pltpu.VMEM((512, width), jnp.bfloat16),
            pltpu.VMEM((total, width), jnp.bfloat16),
            pltpu.VMEM((8, width), jnp.float32),
            pltpu.SemaphoreType.DMA((width // 256,)),
        ],
        compiler_params=pltpu.CompilerParams(vmem_limit_bytes=50 * 1024 * 1024),
        name="gram",
    )(emb, inverse)
    return (
        trailing.reshape(n_col, 1, stretch, n_row, 1, stretch),
        own_factor.reshape(1, 1, stretch, width),
    )


def solution(mesh):
    return jax.shard_map(
        shards,
        mesh=mesh,
        in_specs=(P(), P("col"), P("row", "col", None), P()),
        out_specs=(P(None, "row", None, None, "col", None), P("row", "col", None, None)),
        check_vma=False,
    )
```

profile of v0, /device:TPU:0, one launch (start us, length us, event | category | flops | bytes accessed | tf_op | source)
XLA Modules:
  0.0 34.4 jit_solution(17586242803317331084)
XLA Ops:
  0.6 0.0 copy-start
  0.6 0.7 %copy-done = s32[256]{0:T(256)S(1)} copy-done((s32[256]{0:T(256)S(1)}, s32[256]{0:T(256)}, u32[]{:S(2)}) %copy-start) | copy-done | bytes 1048
  1.3 0.0 copy-start.1
  1.3 0.7 %copy-done.1 = s32[1,1,128]{2,1,0:T(1,128)S(1)} copy-done((s32[1,1,128]{2,1,0:T(1,128)S(1)}, s32[1,1,128]{2,1,0:T(1,128)}, u32[]{:S(2)}) %copy-start.1) | copy-done | bytes 536
  2.0 15.3 %exchange.1.emb_ref = bf16[3584,256]{1,0:T(8,128)(2,1)S(1)} custom-call(s32[1,1,128]{2,1,0:T(1,128)S(1)} %copy-done.1, s32[1,1,256]{2,1,0:T(1,128)S(1)} %bitcast.5, bf16[16384,256]{1,0:T(8,128)(2,1)} %table_hbm.1), custom_call_target="tpu_custom_call" | custom-call | tf_op jit(solution)/shard_map/exchange/pallas_call | solution.py:139
  17.3 17.1 %gram.1 = (f32[4096,128]{1,0:T(8,128)}, bf16[128,2048]{1,0:T(8,128)(2,1)}) custom-call(bf16[3584,256]{1,0:T(8,128)(2,1)S(1)} %exchange.1.emb_ref, bf16[2048,2048]{1,0:T(8,128)(2,1)} %inv_hbm.1), custom_call_target="tpu_custom_call" | custom-call | tf_op jit(solution)/shard_map/gram/pallas_call | solution.py:261
Async XLA Ops:
  0.6 0.7 %copy-start = (s32[256]{0:T(256)S(1)}, s32[256]{0:T(256)}, u32[]{:S(2)}) copy-start(s32[256]{0:T(256)} %param.5) | copy-start | bytes 3076
  1.3 0.7 %copy-start.1 = (s32[1,1,128]{2,1,0:T(1,128)S(1)}, s32[1,1,128]{2,1,0:T(1,128)}, u32[]{:S(2)}) copy-start(s32[1,1,128]{2,1,0:T(1,128)} %rest_ref.1) | copy-start | bytes 1540
where the time goes:
time: 34.5 us; the launch traced here: 34.4 us
  Pallas kernels  32.4 us (94%)
  local copies, waits for them, and re-layouts  1.33 us (4%)
  between operations  0.65 us (2%)
    pallas_call x1, Pallas kernels, shards(): pl.pallas_call(functools.partial(gram_kernel, n_row, n_col, stretch), out...  17.1 us
    pallas_call x1, Pallas kernels, exchange(): pl.pallas_call(functools.partial(exchange_kernel, n_row, n_col), out_shap...  15.3 us
    unnamed x4, local copies, waits for them, and re-layouts  1.33 us

commit v1 on v0

v1 whole, which is shorter than its diff:
```python
import functools

import jax
import jax.numpy as jnp
from jax import lax
from jax.experimental import pallas as pl
from jax.experimental.pallas import tpu as pltpu
from jax.sharding import PartitionSpec as P

MESH = pl.DeviceIdType.MESH
LANES = 128
VMEM_BYTES = 67043328


def narrow(picked, out, first, count, at):
    halves = out.shape[1] // LANES
    for step in range(0, count, 64):
        for half in range(halves):
            value = picked[pl.ds((first + step) * halves + half, 64, stride=halves), :]
            out[at + step : at + step + 64, half * LANES : (half + 1) * LANES] = value.astype(jnp.bfloat16)


def exchange_kernel(
    n_row, n_col, rest_hbm, panel_hbm, table_hbm, emb_ref, table_ref, rows_out,
    panel_land, col_land, row_land, panel_scaled, col_scaled, panel_ids, col_ids, landed, picked,
    panel_send, row_send, col_send, panel_sem, row_sem, col_sem, table_sem, own_sem, ids_sem,
):
    pieces = table_sem.shape[0]
    halves = table_hbm.shape[1] // LANES
    piece = table_hbm.shape[0] // pieces
    width = panel_land.shape[2]
    stretch = col_land.shape[2]
    row_at = lax.axis_index("row")
    col_at = lax.axis_index("col")
    group = col_at // n_row
    forwards = lax.rem(col_at, n_row) == row_at

    own_panel = pltpu.make_async_copy(panel_hbm.at[0], panel_land.at[col_at], own_sem.at[0])
    own_col = pltpu.make_async_copy(rest_hbm.at[0], col_land.at[row_at], own_sem.at[1])
    own_panel.start()
    own_col.start()

    def load(at):
        rows = pl.ds(at * piece, piece)
        return pltpu.make_async_copy(table_hbm.at[rows], landed.at[rows], table_sem.at[at])

    for at in range(pieces):
        load(at).start()
    barrier = pltpu.get_barrier_semaphore()
    for step in range(1, n_row):
        other = lax.rem(row_at + step, n_row)
        pl.semaphore_signal(barrier, inc=1, device_id=(other, col_at), device_id_type=MESH)
    for step in range(1, n_col):
        other = lax.rem(col_at + step, n_col)
        pl.semaphore_signal(barrier, inc=1, device_id=(row_at, other), device_id_type=MESH)

    def widen(at):
        def body(step, carry):
            rows = pl.ds(pl.multiple_of(at * piece + step * 64, 64), 64)
            wide = landed[rows, :].astype(jnp.float32)
            for half in range(halves):
                place = pl.ds((at * piece + step * 64) * halves + half, 64, stride=halves)
                table_ref[place, :] = wide[:, half * LANES : (half + 1) * LANES]
            return carry

        load(at).wait()
        lax.fori_loop(0, piece // 64, body, 0)

    def panel_copy(slot, target):
        return pltpu.make_async_remote_copy(
            src_ref=panel_land.at[slot], dst_ref=panel_land.at[slot],
            send_sem=panel_send.at[target], recv_sem=panel_sem.at[slot],
            device_id=(row_at, target), device_id_type=MESH,
        )

    def row_copy(slot, target):
        return pltpu.make_async_remote_copy(
            src_ref=col_land, dst_ref=row_land.at[slot],
            send_sem=row_send.at[target], recv_sem=row_sem.at[slot],
            device_id=(row_at, target), device_id_type=MESH,
        )

    def col_copy(slot, target):
        return pltpu.make_async_remote_copy(
            src_ref=col_land.at[slot], dst_ref=col_land.at[slot],
            send_sem=col_send.at[target], recv_sem=col_sem.at[slot],
            device_id=(target, col_at), device_id_type=MESH,
        )

    def each(length, skip, act):
        for at in range(length):
            pl.when(jnp.logical_not(skip(at)))(functools.partial(act, at))

    own_panel.wait()
    own_col.wait()
    pl.semaphore_wait(barrier, n_row + n_col - 2)
    each(n_row, lambda at: at == row_at, lambda at: col_copy(row_at, at).start())
    each(n_col, lambda at: at == col_at, lambda at: panel_copy(col_at, at).start())
    for at in range(pieces):
        widen(at)
    each(n_row, lambda at: at == row_at, lambda at: col_copy(at, at).wait_recv())
    keep = pltpu.make_async_copy(col_land, row_land.at[group], own_sem.at[0])

    @pl.when(forwards)
    def _():
        each(n_col, lambda at: at == col_at, lambda at: row_copy(group, at).start())
        keep.start()

    col_scaled[...] = col_land[...] * halves
    col_move = pltpu.make_async_copy(col_scaled, col_ids, ids_sem.at[0])
    col_move.start()
    each(n_col, lambda at: at == col_at, lambda at: panel_copy(at, at).wait_recv())
    panel_scaled[...] = panel_land[...] * halves
    panel_move = pltpu.make_async_copy(panel_scaled, panel_ids, ids_sem.at[1])
    panel_move.start()

    def pick(ids, block, span, start):
        for lane in range(span):
            place = (start + lane) * halves
            picked[place : place + halves, :] = table_ref[pl.ds(ids[block, 0, lane], halves), :]

    col_move.wait()
    first_col = n_col * width
    for block in range(n_row):
        pick(col_ids, block, stretch, first_col + block * stretch)
    narrow(picked, emb_ref, first_col, n_row * stretch, first_col)
    panel_move.wait()
    for block in range(n_col):
        pick(panel_ids, block, width, block * width)
        if block:
            narrow(picked, emb_ref, (block - 1) * width, width, (block - 1) * width)
    narrow(picked, emb_ref, (n_col - 1) * width, width, (n_col - 1) * width)

    @pl.when(forwards)
    def _():
        keep.wait()

    for slot in range(n_col // n_row):
        source = slot * n_row + row_at

        @pl.when(source != col_at)
        def _(slot=slot, source=source):
            row_copy(slot, source).wait_recv()

    rows_out[...] = row_land[...] * halves
    each(n_row, lambda at: at == row_at, lambda at: col_copy(row_at, at).wait_send())
    each(n_col, lambda at: at == col_at, lambda at: panel_copy(col_at, at).wait_send())

    @pl.when(forwards)
    def _():
        each(n_col, lambda at: at == col_at, lambda at: row_copy(group, at).wait_send())


def exchange(rest_ids, panel_ids, teacher, n_row, n_col):
    stretch = rest_ids.shape[2]
    width = panel_ids.shape[0]
    total = n_col * width + n_row * stretch
    halves = teacher.shape[1] // LANES
    groups = n_col // n_row
    panel_shape = (n_col, 1, width)
    col_shape = (n_row, 1, stretch)
    row_shape = (groups, n_row, 1, stretch)
    vmem = pl.BlockSpec(memory_space=pltpu.VMEM)
    hbm = pl.BlockSpec(memory_space=pltpu.HBM)
    dma = pltpu.SemaphoreType.DMA
    limit = VMEM_BYTES - 4 * teacher.size - 2 * total * teacher.shape[1] - 12 * 1024 * 1024
    return pl.pallas_call(
        functools.partial(exchange_kernel, n_row, n_col),
        out_shape=(
            jax.ShapeDtypeStruct((total, teacher.shape[1]), teacher.dtype),
            jax.ShapeDtypeStruct((teacher.shape[0] * halves, LANES), jnp.float32),
            jax.ShapeDtypeStruct(row_shape, jnp.int32),
        ),
        in_specs=[hbm, hbm, hbm],
        out_specs=(vmem, vmem, vmem),
        scratch_shapes=[
            pltpu.VMEM(panel_shape, jnp.int32),
            pltpu.VMEM(col_shape, jnp.int32),
            pltpu.VMEM(row_shape, jnp.int32),
            pltpu.VMEM(panel_shape, jnp.int32),
            pltpu.VMEM(col_shape, jnp.int32),
            pltpu.SMEM(panel_shape, jnp.int32),
            pltpu.SMEM(col_shape, jnp.int32),
            pltpu.VMEM(teacher.shape, teacher.dtype),
            pltpu.VMEM((total * halves, LANES), jnp.float32),
            dma((n_col,)), dma((n_col,)), dma((n_row,)),
            dma((n_col,)), dma((groups,)), dma((n_row,)),
            dma((8,)), dma((2,)), dma((2,)),
        ],
        compiler_params=pltpu.CompilerParams(
            collective_id=0, has_side_effects=True, vmem_limit_bytes=limit
        ),
        name="exchange",
    )(*(pltpu.with_memory_space_constraint(x, pltpu.HBM) for x in (rest_ids, panel_ids.reshape(1, 1, width), teacher)))


def nt_dot(left, right):
    return lax.dot_general(left, right, (((1,), (1,)), ((), ())), preferred_element_type=jnp.float32)


def nn_dot(left, right):
    return lax.dot_general(left, right, (((1,), (0,)), ((), ())), preferred_element_type=jnp.float32)


def gram_kernel(
    n_row, n_col, stretch, emb_ref, rows_in, table_ref, inv_hbm, trail_hbm, own_hbm,
    row_ids, picked, left_ref, inv_ref, cross_ref, fac_ref, back_ref, norm_ref, trail_ref,
    inv_sem, ids_sem, own_sem, trail_sem,
):
    width = inv_hbm.shape[0]
    block = 256
    blocks = width // block
    embed = emb_ref.shape[1]
    halves = embed // LANES
    n_rows = n_col * stretch
    n_cols = n_row * stretch
    groups = n_col // n_row
    unit = 2.0 / embed * 1.4426950408889634
    row_at = lax.axis_index("row")
    col_at = lax.axis_index("col")
    tile = 512

    ids_move = pltpu.make_async_copy(rows_in, row_ids, ids_sem)
    ids_move.start()

    def load(at):
        rows, cols = pl.ds(at * block, block), pl.ds(0, (at + 1) * block)
        return pltpu.make_async_copy(inv_hbm.at[rows, cols], inv_ref.at[rows, cols], inv_sem.at[at])

    for at in range(blocks):
        load(at).start()

    eye = lax.broadcasted_iota(jnp.int32, (LANES, LANES), 0) == lax.broadcasted_iota(jnp.int32, (LANES, LANES), 1)

    def down(value):
        return jnp.sum(jnp.square(value.astype(jnp.float32)), axis=-1, keepdims=True) * unit

    def across(start, count):
        for at in range(start, start + count, LANES):
            norm = jnp.broadcast_to(down(emb_ref[at : at + LANES, :]), (LANES, LANES))
            norm_ref[0:1, at : at + LANES] = jnp.sum(jnp.where(eye, norm, 0.0), axis=0, keepdims=True)

    def gram(left, left_norm, start, count):
        right, right_norm = emb_ref[start : start + count, :], norm_ref[0:1, start : start + count]
        return jnp.exp2(nt_dot(left, right) * (2.0 * unit) - (left_norm + right_norm))

    def pick(start, count):
        for row in range(start, start + count):
            q, lane = divmod(row, stretch)
            place = table_ref[pl.ds(row_ids[q % groups, q // groups, 0, lane], halves), :]
            picked[row * halves : (row + 1) * halves, :] = place
        narrow(picked, left_ref, start, count, start)

    share = n_rows * tile // (n_cols * blocks)
    ids_move.wait()
    done = 0
    for start in range(0, n_cols, tile):
        left = emb_ref[width + start : width + start + tile, :]
        left_norm = down(left)
        rows = slice(start, start + tile)
        for at in range(blocks):
            cols = slice(at * block, (at + 1) * block)
            if not start:
                across(at * block, block)
            cross_ref[:, cols] = gram(left, left_norm, at * block, block).astype(jnp.bfloat16)
            if not start:
                load(at).wait()
            fac_ref[rows, cols] = nt_dot(
                cross_ref[:, : (at + 1) * block], inv_ref[cols, : (at + 1) * block]
            ).astype(jnp.bfloat16)
            pick(done, share)
            done += share
    own = pltpu.make_async_copy(
        fac_ref.at[pl.ds(pl.multiple_of(row_at * stretch, stretch), stretch), :], own_hbm, own_sem
    )
    own.start()
    across(width, n_cols)
    for start in range(0, n_cols, tile):
        rows = slice(start, start + tile)
        for at in range(blocks):
            cols = slice(at * block, (at + 1) * block)
            back_ref[rows, cols] = nn_dot(fac_ref[rows, at * block :], inv_ref[at * block :, cols]).astype(jnp.bfloat16)

    ahead = lax.broadcasted_iota(jnp.int32, (stretch, stretch), 0) - lax.broadcasted_iota(
        jnp.int32, (stretch, stretch), 1
    )
    pair = 2 if n_row % 2 == 0 else 1

    def flush(start):
        first, count = start // stretch, tile // stretch
        span = pl.ds(first * stretch * n_row, count * stretch * n_row)
        return pltpu.make_async_copy(trail_ref.at[span], trail_hbm.at[span], trail_sem.at[start // tile])

    for start in range(0, n_rows, tile):
        left = left_ref[start : start + tile, :]
        left_norm = down(left)
        last = (start + tile) // stretch - 1
        for at in range(blocks):
            cross_ref[:, at * block : (at + 1) * block] = gram(left, left_norm, at * block, block).astype(jnp.bfloat16)
        for low in range(0, n_row, pair):
            if last * n_row + n_row - 1 >= low * n_col:
                span = slice(low * stretch, (low + pair) * stretch)
                value = gram(left, left_norm, width + low * stretch, pair * stretch) - nt_dot(
                    cross_ref[...], back_ref[span, :]
                )
            else:
                value = None
            for q in range(start // stretch, last + 1):
                for p in range(low, low + pair):
                    place = pl.ds(q * stretch * n_row + p, stretch, stride=n_row)
                    if q * n_row + n_row - 1 < p * n_col:
                        trail_ref[place, :] = jnp.zeros((stretch, stretch), jnp.float32)
                    else:
                        top = q * stretch - start
                        side = (p - low) * stretch
                        part = value[top : top + stretch, side : side + stretch]
                        gap = (p * n_col + col_at - q * n_row - row_at) * stretch
                        trail_ref[place, :] = jnp.where(ahead >= gap, part, 0.0)
        flush(start).start()
    own.wait()
    for start in range(0, n_rows, tile):
        flush(start).wait()


def shards(teacher, panel_ids, rest_ids, inverse):
    n_row = lax.axis_size("row")
    n_col = lax.axis_size("col")
    stretch = rest_ids.shape[2]
    width = inverse.shape[0]
    emb, table, rows = exchange(rest_ids, panel_ids, teacher, n_row, n_col)
    n_rows = n_col * stretch
    n_cols = n_row * stretch
    embed = teacher.shape[1]
    halves = embed // LANES
    vmem = pl.BlockSpec(memory_space=pltpu.VMEM)
    hbm = pl.BlockSpec(memory_space=pltpu.HBM)
    dma = pltpu.SemaphoreType.DMA
    limit = VMEM_BYTES - 4 * teacher.size - 2 * (width + n_cols) * embed - 12 * 1024 * 1024
    trailing, own_factor = pl.pallas_call(
        functools.partial(gram_kernel, n_row, n_col, stretch),
        out_shape=(
            jax.ShapeDtypeStruct((n_rows * n_row, stretch), jnp.float32),
            jax.ShapeDtypeStruct((stretch, width), jnp.bfloat16),
        ),
        in_specs=[vmem, vmem, vmem, hbm],
        out_specs=(hbm, hbm),
        scratch_shapes=[
            pltpu.SMEM(rows.shape, jnp.int32),
            pltpu.VMEM((n_rows * halves, LANES), jnp.float32),
            pltpu.VMEM((n_rows, embed), jnp.bfloat16),
            pltpu.VMEM((width, width), jnp.bfloat16),
            pltpu.VMEM((512, width), jnp.bfloat16),
            pltpu.VMEM((n_cols, width), jnp.bfloat16),
            pltpu.VMEM((n_cols, width), jnp.bfloat16),
            pltpu.VMEM((8, width + n_cols), jnp.float32),
            pltpu.VMEM((n_rows * n_row, stretch), jnp.float32),
            dma((width // 256,)), dma(()), dma(()), dma((n_rows // 512,)),
        ],
        compiler_params=pltpu.CompilerParams(vmem_limit_bytes=limit),
        name="gram",
    )(emb, rows, table, pltpu.with_memory_space_constraint(inverse, pltpu.HBM))
    return (
        trailing.reshape(n_col, 1, stretch, n_row, 1, stretch),
        own_factor.reshape(1, 1, stretch, width),
    )


def solution(mesh):
    return jax.shard_map(
        shards,
        mesh=mesh,
        in_specs=(P(), P("col"), P("row", "col", None), P()),
        out_specs=(P(None, "row", None, None, "col", None), P("row", "col", None, None)),
        check_vma=False,
    )
```

time: 34.5 us -> 28.5 us (0.83)
  Pallas kernels: 32.4 us -> 27.7 us
  local copies, waits for them, and re-layouts: 1.33 us -> 0 us
    pallas_call x1, Pallas kernels: 17.1 us -> 14.5 us  [shards(): pl.pallas_call(functools.partial(gram_kernel, n_row, n_col, stretch), out...]
    pallas_call x1, Pallas kernels: 15.3 us -> 13.2 us  [exchange(): pl.pallas_call(functools.partial(exchange_kernel, n_row, n_col), out_shap...]
    unnamed x4 -> x0, local copies, waits for them, and re-layouts: 1.33 us -> none
where the time goes in v1:
time: 28.5 us; the launch traced here: 28.4 us
  Pallas kernels  27.7 us (97%)
  between operations  0.64 us (2%)
    pallas_call x1, Pallas kernels, shards(): pl.pallas_call(functools.partial(gram_kernel, n_row, n_col, stretch), out...  14.5 us
    pallas_call x1, Pallas kernels, exchange(): pl.pallas_call(functools.partial(exchange_kernel, n_row, n_col), out_shap...  13.2 us

profile of v1, /device:TPU:0, one launch (start us, length us, event | category | flops | bytes accessed | tf_op | source)
XLA Modules:
  0.0 28.4 jit_solution(11313112684192463535)
XLA Ops:
  0.6 13.2 %exchange.1 = (bf16[2560,256]{1,0:T(8,128)(2,1)S(1)}, f32[32768,128]{1,0:T(8,128)S(1)}, s32[2,4,1,128]{3,2,1,0:T(1,128)S(1)}) custom-call(s32[1,1,128]{2,1,0:T(1,128)} %rest_hbm.1, s32[1,1,256]{2,1,0:T(1,128)} %bitcast.5, bf16[16384,256]{1,0:T(8,128)(2,1)} %table_hbm.1), custom_call_target="tpu_custom_call" | custom-call | tf_op jit(solution)/shard_map/exchange/pallas_call | solution.py:167
  13.8 14.5 %gram.1 = (f32[4096,128]{1,0:T(8,128)}, bf16[128,2048]{1,0:T(8,128)(2,1)}) custom-call(bf16[2560,256]{1,0:T(8,128)(2,1)S(1)} %get-tuple-element.7.emb_ref, s32[2,4,1,128]{3,2,1,0:T(1,128)S(1)} %get-tuple-element.8.rows_in, f32[32768,128]{1,0:T(8,128)S(1)} %get-tuple-element.9.table_ref, bf16[2048,2048]{1,0:T(8,128)(2,1)} %inv_hbm.1), custom_call_target="tpu_custom_call" | custom-call | tf_op jit(solution)/shard_map/gram/pallas_call | solution.py:339

commit v2 on v1

--- a/solution.py
+++ b/solution.py
@@ -21,9 +21,9 @@
 
 
 def exchange_kernel(
-    n_row, n_col, rest_hbm, panel_hbm, table_hbm, emb_ref, table_ref, rows_out,
+    n_row, n_col, rest_hbm, panel_hbm, table_hbm, inv_hbm, emb_ref, table_ref, rows_out, inv_ref,
     panel_land, col_land, row_land, panel_scaled, col_scaled, panel_ids, col_ids, landed, picked,
-    panel_send, row_send, col_send, panel_sem, row_sem, col_sem, table_sem, own_sem, ids_sem,
+    panel_send, row_send, col_send, panel_sem, row_sem, col_sem, table_sem, inv_sem, own_sem, ids_sem,
 ):
     pieces = table_sem.shape[0]
     halves = table_hbm.shape[1] // LANES
@@ -44,8 +44,15 @@
         rows = pl.ds(at * piece, piece)
         return pltpu.make_async_copy(table_hbm.at[rows], landed.at[rows], table_sem.at[at])
 
+    def load_inverse(at):
+        block = inv_hbm.shape[0] // pieces
+        rows, cols = pl.ds(at * block, block), pl.ds(0, (at + 1) * block)
+        return pltpu.make_async_copy(inv_hbm.at[rows, cols], inv_ref.at[rows, cols], inv_sem.at[at])
+
     for at in range(pieces):
         load(at).start()
+    for at in range(pieces):
+        load_inverse(at).start()
     barrier = pltpu.get_barrier_semaphore()
     for step in range(1, n_row):
         other = lax.rem(row_at + step, n_row)
@@ -143,6 +150,8 @@
             row_copy(slot, source).wait_recv()
 
     rows_out[...] = row_land[...] * halves
+    for at in range(pieces):
+        load_inverse(at).wait()
     each(n_row, lambda at: at == row_at, lambda at: col_copy(row_at, at).wait_send())
     each(n_col, lambda at: at == col_at, lambda at: panel_copy(col_at, at).wait_send())
 
@@ -151,7 +160,11 @@
         each(n_col, lambda at: at == col_at, lambda at: row_copy(group, at).wait_send())
 
 
-def exchange(rest_ids, panel_ids, teacher, n_row, n_col):
+def own_limit(teacher, inverse, total):
+    return VMEM_BYTES - 4 * teacher.size - 2 * inverse.size - 2 * total * teacher.shape[1] - 12 * 1024 * 1024
+
+
+def exchange(rest_ids, panel_ids, teacher, inverse, n_row, n_col):
     stretch = rest_ids.shape[2]
     width = panel_ids.shape[0]
     total = n_col * width + n_row * stretch
@@ -163,16 +176,17 @@
     vmem = pl.BlockSpec(memory_space=pltpu.VMEM)
     hbm = pl.BlockSpec(memory_space=pltpu.HBM)
     dma = pltpu.SemaphoreType.DMA
-    limit = VMEM_BYTES - 4 * teacher.size - 2 * total * teacher.shape[1] - 12 * 1024 * 1024
+    operands = (rest_ids, panel_ids.reshape(1, 1, width), teacher, inverse)
     return pl.pallas_call(
         functools.partial(exchange_kernel, n_row, n_col),
         out_shape=(
             jax.ShapeDtypeStruct((total, teacher.shape[1]), teacher.dtype),
             jax.ShapeDtypeStruct((teacher.shape[0] * halves, LANES), jnp.float32),
             jax.ShapeDtypeStruct(row_shape, jnp.int32),
+            jax.ShapeDtypeStruct(inverse.shape, inverse.dtype),
         ),
-        in_specs=[hbm, hbm, hbm],
-        out_specs=(vmem, vmem, vmem),
+        in_specs=[hbm] * 4,
+        out_specs=(vmem,) * 4,
         scratch_shapes=[
             pltpu.VMEM(panel_shape, jnp.int32),
             pltpu.VMEM(col_shape, jnp.int32),
@@ -185,13 +199,13 @@
             pltpu.VMEM((total * halves, LANES), jnp.float32),
             dma((n_col,)), dma((n_col,)), dma((n_row,)),
             dma((n_col,)), dma((groups,)), dma((n_row,)),
-            dma((8,)), dma((2,)), dma((2,)),
+            dma((8,)), dma((8,)), dma((2,)), dma((2,)),
         ],
         compiler_params=pltpu.CompilerParams(
-            collective_id=0, has_side_effects=True, vmem_limit_bytes=limit
+            collective_id=0, has_side_effects=True, vmem_limit_bytes=own_limit(teacher, inverse, total)
         ),
         name="exchange",
-    )(*(pltpu.with_memory_space_constraint(x, pltpu.HBM) for x in (rest_ids, panel_ids.reshape(1, 1, width), teacher)))
+    )(*(pltpu.with_memory_space_constraint(x, pltpu.HBM) for x in operands))
 
 
 def nt_dot(left, right):
@@ -203,11 +217,11 @@
 
 
 def gram_kernel(
-    n_row, n_col, stretch, emb_ref, rows_in, table_ref, inv_hbm, trail_hbm, own_hbm,
-    row_ids, picked, left_ref, inv_ref, cross_ref, fac_ref, back_ref, norm_ref, trail_ref,
-    inv_sem, ids_sem, own_sem, trail_sem,
+    n_row, n_col, stretch, emb_ref, rows_in, table_ref, inv_ref, trail_hbm, own_hbm,
+    row_ids, picked, left_ref, cross_ref, fac_ref, back_ref, norm_ref, trail_ref,
+    ids_sem, own_sem, trail_sem,
 ):
-    width = inv_hbm.shape[0]
+    width = inv_ref.shape[0]
     block = 256
     blocks = width // block
     embed = emb_ref.shape[1]
@@ -219,17 +233,11 @@
     row_at = lax.axis_index("row")
     col_at = lax.axis_index("col")
     tile = 512
+    chunk = 64
+    ring = picked.shape[0] // (chunk * halves)
 
     ids_move = pltpu.make_async_copy(rows_in, row_ids, ids_sem)
     ids_move.start()
-
-    def load(at):
-        rows, cols = pl.ds(at * block, block), pl.ds(0, (at + 1) * block)
-        return pltpu.make_async_copy(inv_hbm.at[rows, cols], inv_ref.at[rows, cols], inv_sem.at[at])
-
-    for at in range(blocks):
-        load(at).start()
-
     eye = lax.broadcasted_iota(jnp.int32, (LANES, LANES), 0) == lax.broadcasted_iota(jnp.int32, (LANES, LANES), 1)
 
     def down(value):
@@ -240,86 +248,116 @@
             norm = jnp.broadcast_to(down(emb_ref[at : at + LANES, :]), (LANES, LANES))
             norm_ref[0:1, at : at + LANES] = jnp.sum(jnp.where(eye, norm, 0.0), axis=0, keepdims=True)
 
-    def gram(left, left_norm, start, count):
-        right, right_norm = emb_ref[start : start + count, :], norm_ref[0:1, start : start + count]
-        return jnp.exp2(nt_dot(left, right) * (2.0 * unit) - (left_norm + right_norm))
+    def inner(left, start, count):
+        return nt_dot(left, emb_ref[start : start + count, :])
+
+    def gaussian(product, left_norm, start, count):
+        return jnp.exp2(product * (2.0 * unit) - (left_norm + norm_ref[0:1, start : start + count]))
 
     def pick(start, count):
-        for row in range(start, start + count):
-            q, lane = divmod(row, stretch)
-            place = table_ref[pl.ds(row_ids[q % groups, q // groups, 0, lane], halves), :]
-            picked[row * halves : (row + 1) * halves, :] = place
-        narrow(picked, left_ref, start, count, start)
-
-    share = n_rows * tile // (n_cols * blocks)
-    ids_move.wait()
-    done = 0
+        for base in range(start, start + count, chunk):
+            home = base // chunk % ring * chunk
+            for lane in range(chunk):
+                q, place = divmod(base + lane, stretch)
+                row = table_ref[pl.ds(row_ids[q % groups, q // groups, 0, place], halves), :]
+                picked[(home + lane) * halves : (home + lane + 1) * halves, :] = row
+            narrow(picked, left_ref, home, chunk, base)
+
+    picked_rows = 0
+    hold = slice(tile, 2 * tile)
     for start in range(0, n_cols, tile):
         left = emb_ref[width + start : width + start + tile, :]
         left_norm = down(left)
         rows = slice(start, start + tile)
-        for at in range(blocks):
-            cols = slice(at * block, (at + 1) * block)
-            if not start:
-                across(at * block, block)
-            cross_ref[:, cols] = gram(left, left_norm, at * block, block).astype(jnp.bfloat16)
-            if not start:
-                load(at).wait()
-            fac_ref[rows, cols] = nt_dot(
-                cross_ref[:, : (at + 1) * block], inv_ref[cols, : (at + 1) * block]
-            ).astype(jnp.bfloat16)
-            pick(done, share)
-            done += share
+        product = inner(left, 0, block)
+        for at in range(blocks + 1):
+            cols = slice((at - 1) * block, at * block)
+            held = product
+            if at < blocks:
+                here = slice(at * block, (at + 1) * block)
+                if not start:
+                    across(at * block, block)
+                cross_ref[hold, here] = gaussian(held, left_norm, at * block, block).astype(jnp.bfloat16)
+                if at + 1 < blocks:
+                    product = inner(left, (at + 1) * block, block)
+            if at:
+                if at == 1 and not start:
+                    ids_move.wait()
+                fac_ref[rows, cols] = nt_dot(
+                    cross_ref[hold, : at * block], inv_ref[cols, : at * block]
+                ).astype(jnp.bfloat16)
+                if not start:
+                    until = n_rows * at * (at + 1) // (blocks * (blocks + 1)) // chunk * chunk
+                    pick(picked_rows, until - picked_rows)
+                    picked_rows = until
     own = pltpu.make_async_copy(
         fac_ref.at[pl.ds(pl.multiple_of(row_at * stretch, stretch), stretch), :], own_hbm, own_sem
     )
     own.start()
     across(width, n_cols)
-    for start in range(0, n_cols, tile):
-        rows = slice(start, start + tile)
-        for at in range(blocks):
-            cols = slice(at * block, (at + 1) * block)
+    lefts = [(start, down(left_ref[start : start + tile, :])) for start in range(0, n_rows, tile)]
+
+    def cross_rows(tile_at, at):
+        start, left_norm = lefts[tile_at]
+        product = inner(left_ref[start : start + tile, :], at * block, block)
+        value = gaussian(product, left_norm, at * block, block)
+        home = tile_at % 2 * tile
+        cross_ref[home : home + tile, at * block : (at + 1) * block] = value.astype(jnp.bfloat16)
+
+    for at in range(blocks):
+        cols = slice(at * block, (at + 1) * block)
+        for tile_at in range(min(2, len(lefts))):
+            cross_rows(tile_at, at)
+        for start in range(0, n_cols, tile):
+            rows = slice(start, start + tile)
             back_ref[rows, cols] = nn_dot(fac_ref[rows, at * block :], inv_ref[at * block :, cols]).astype(jnp.bfloat16)
 
     ahead = lax.broadcasted_iota(jnp.int32, (stretch, stretch), 0) - lax.broadcasted_iota(
         jnp.int32, (stretch, stretch), 1
     )
     pair = 2 if n_row % 2 == 0 else 1
-
-    def flush(start):
-        first, count = start // stretch, tile // stretch
-        span = pl.ds(first * stretch * n_row, count * stretch * n_row)
-        return pltpu.make_async_copy(trail_ref.at[span], trail_hbm.at[span], trail_sem.at[start // tile])
-
-    for start in range(0, n_rows, tile):
+    held_rows = tile * n_row
+
+    def flush(at):
+        return pltpu.make_async_copy(
+            trail_ref.at[pl.ds(at % 2 * held_rows, held_rows)], trail_hbm.at[pl.ds(at * held_rows, held_rows)],
+            trail_sem.at[at % 2],
+        )
+
+    for tile_at, (start, left_norm) in enumerate(lefts):
         left = left_ref[start : start + tile, :]
-        left_norm = down(left)
         last = (start + tile) // stretch - 1
-        for at in range(blocks):
-            cross_ref[:, at * block : (at + 1) * block] = gram(left, left_norm, at * block, block).astype(jnp.bfloat16)
+        if tile_at >= 2:
+            flush(tile_at - 2).wait()
+            for at in range(blocks):
+                cross_rows(tile_at, at)
+        home = tile_at % 2 * tile
         for low in range(0, n_row, pair):
             if last * n_row + n_row - 1 >= low * n_col:
                 span = slice(low * stretch, (low + pair) * stretch)
-                value = gram(left, left_norm, width + low * stretch, pair * stretch) - nt_dot(
-                    cross_ref[...], back_ref[span, :]
+                first = width + low * stretch
+                value = gaussian(inner(left, first, pair * stretch), left_norm, first, pair * stretch) - nt_dot(
+                    cross_ref[home : home + tile, :], back_ref[span, :]
                 )
             else:
                 value = None
             for q in range(start // stretch, last + 1):
                 for p in range(low, low + pair):
-                    place = pl.ds(q * stretch * n_row + p, stretch, stride=n_row)
+                    top = q * stretch - start
+                    place = pl.ds(tile_at % 2 * held_rows + top * n_row + p, stretch, stride=n_row)
                     if q * n_row + n_row - 1 < p * n_col:
                         trail_ref[place, :] = jnp.zeros((stretch, stretch), jnp.float32)
-                    else:
-                        top = q * stretch - start
-                        side = (p - low) * stretch
-                        part = value[top : top + stretch, side : side + stretch]
+                        continue
+                    side = (p - low) * stretch
+                    part = value[top : top + stretch, side : side + stretch]
+                    if q * n_row < p * n_col + n_col:
                         gap = (p * n_col + col_at - q * n_row - row_at) * stretch
-                        trail_ref[place, :] = jnp.where(ahead >= gap, part, 0.0)
-        flush(start).start()
+                        part = jnp.where(ahead >= gap, part, 0.0)
+                    trail_ref[place, :] = part
+        flush(tile_at).start()
     own.wait()
-    for start in range(0, n_rows, tile):
-        flush(start).wait()
+    for tile_at in range(max(len(lefts) - 2, 0), len(lefts)):
+        flush(tile_at).wait()
 
 
 def shards(teacher, panel_ids, rest_ids, inverse):
@@ -327,7 +365,7 @@
     n_col = lax.axis_size("col")
     stretch = rest_ids.shape[2]
     width = inverse.shape[0]
-    emb, table, rows = exchange(rest_ids, panel_ids, teacher, n_row, n_col)
+    emb, table, rows, inv = exchange(rest_ids, panel_ids, teacher, inverse, n_row, n_col)
     n_rows = n_col * stretch
     n_cols = n_row * stretch
     embed = teacher.shape[1]
@@ -335,30 +373,30 @@
     vmem = pl.BlockSpec(memory_space=pltpu.VMEM)
     hbm = pl.BlockSpec(memory_space=pltpu.HBM)
     dma = pltpu.SemaphoreType.DMA
-    limit = VMEM_BYTES - 4 * teacher.size - 2 * (width + n_cols) * embed - 12 * 1024 * 1024
+    limit = own_limit(teacher, inverse, width + n_cols)
+    held = 2 * n_rows * embed + 2048 * width + 4 * n_cols * width + 4096 * n_row * stretch + 9 * 1024 * 1024
     trailing, own_factor = pl.pallas_call(
         functools.partial(gram_kernel, n_row, n_col, stretch),
         out_shape=(
             jax.ShapeDtypeStruct((n_rows * n_row, stretch), jnp.float32),
             jax.ShapeDtypeStruct((stretch, width), jnp.bfloat16),
         ),
-        in_specs=[vmem, vmem, vmem, hbm],
+        in_specs=[vmem] * 4,
         out_specs=(hbm, hbm),
         scratch_shapes=[
             pltpu.SMEM(rows.shape, jnp.int32),
-            pltpu.VMEM((n_rows * halves, LANES), jnp.float32),
+            pltpu.VMEM((512 * halves, LANES), jnp.float32),
             pltpu.VMEM((n_rows, embed), jnp.bfloat16),
-            pltpu.VMEM((width, width), jnp.bfloat16),
-            pltpu.VMEM((512, width), jnp.bfloat16),
+            pltpu.VMEM((2 * 512, width), jnp.bfloat16),
             pltpu.VMEM((n_cols, width), jnp.bfloat16),
             pltpu.VMEM((n_cols, width), jnp.bfloat16),
             pltpu.VMEM((8, width + n_cols), jnp.float32),
-            pltpu.VMEM((n_rows * n_row, stretch), jnp.float32),
-            dma((width // 256,)), dma(()), dma(()), dma((n_rows // 512,)),
+            pltpu.VMEM((2 * 512 * n_row, stretch), jnp.float32),
+            dma(()), dma(()), dma((2,)),
         ],
-        compiler_params=pltpu.CompilerParams(vmem_limit_bytes=limit),
+        compiler_params=pltpu.CompilerParams(vmem_limit_bytes=max(limit, held)),
         name="gram",
-    )(emb, rows, table, pltpu.with_memory_space_constraint(inverse, pltpu.HBM))
+    )(emb, rows, table, inv)
     return (
         trailing.reshape(n_col, 1, stretch, n_row, 1, stretch),
         own_factor.reshape(1, 1, stretch, width),

time: 28.5 us -> 26.4 us (0.926)
  Pallas kernels: 27.7 us -> 25.7 us
    pallas_call x1, Pallas kernels: 14.5 us -> 11.3 us  [shards(): pl.pallas_call(functools.partial(gram_kernel, n_row, n_col, stretch), out...]
    pallas_call x1, Pallas kernels: 13.2 us -> 14.3 us  [exchange(): pl.pallas_call(functools.partial(exchange_kernel, n_row, n_col), out_shap...]
where the time goes in v2:
time: 26.4 us; the launch traced here: 26.3 us
  Pallas kernels  25.7 us (97%)
  between operations  0.64 us (2%)
    pallas_call x1, Pallas kernels, exchange(): pl.pallas_call(functools.partial(exchange_kernel, n_row, n_col), out_shap...  14.3 us
    pallas_call x1, Pallas kernels, shards(): pl.pallas_call(functools.partial(gram_kernel, n_row, n_col, stretch), out...  11.3 us

profile of v2, /device:TPU:0, one launch (start us, length us, event | category | flops | bytes accessed | tf_op | source)
XLA Modules:
  0.0 26.3 jit_solution(6711395473689384076)
XLA Ops:
  0.6 14.3 %exchange.1 = (bf16[2560,256]{1,0:T(8,128)(2,1)S(1)}, f32[32768,128]{1,0:T(8,128)S(1)}, s32[2,4,1,128]{3,2,1,0:T(1,128)S(1)}, bf16[2048,2048]{1,0:T(8,128)(2,1)S(1)}) custom-call(s32[1,1,128]{2,1,0:T(1,128)} %rest_hbm.1, s32[1,1,256]{2,1,0:T(1,128)} %bitcast.5, bf16[16384,256]{1,0:T(8,128)(2,1)} %table_hbm.1, bf16[2048,2048]{1,0:T(8,128)(2,1)} %inv_hbm.1), custom_call_target="tpu_custom_call" | custom-call | tf_op jit(solution)/shard_map/exchange/pallas_call | solution.py:180
  15.0 11.3 %gram.1 = (f32[4096,128]{1,0:T(8,128)}, bf16[128,2048]{1,0:T(8,128)(2,1)}) custom-call(bf16[2560,256]{1,0:T(8,128)(2,1)S(1)} %get-tuple-element.8.emb_ref, s32[2,4,1,128]{3,2,1,0:T(1,128)S(1)} %get-tuple-element.9.rows_in, f32[32768,128]{1,0:T(8,128)S(1)} %get-tuple-element.10.table_ref, bf16[2048,2048]{1,0:T(8,128)(2,1)S(1)} %get-tuple-element.11.inv_ref), custom_call_target="tpu_custom_call" | custom-call | tf_op jit(solution)/shard_map/gram/pallas_call | solution.py:378

commit v3 on v2

--- a/solution.py
+++ b/solution.py
@@ -20,8 +20,16 @@
             out[at + step : at + step + 64, half * LANES : (half + 1) * LANES] = value.astype(jnp.bfloat16)
 
 
+def unit_of(embed):
+    return 2.0 / embed * 1.4426950408889634
+
+
+def row_norm(value):
+    return jnp.sum(jnp.square(value.astype(jnp.float32)), axis=-1, keepdims=True) * unit_of(value.shape[1])
+
+
 def exchange_kernel(
-    n_row, n_col, rest_hbm, panel_hbm, table_hbm, inv_hbm, emb_ref, table_ref, rows_out, inv_ref,
+    n_row, n_col, rest_hbm, panel_hbm, table_hbm, inv_hbm, emb_ref, table_ref, rows_out, inv_ref, norm_ref,
     panel_land, col_land, row_land, panel_scaled, col_scaled, panel_ids, col_ids, landed, picked,
     panel_send, row_send, col_send, panel_sem, row_sem, col_sem, table_sem, inv_sem, own_sem, ids_sem,
 ):
@@ -51,8 +59,6 @@
 
     for at in range(pieces):
         load(at).start()
-    for at in range(pieces):
-        load_inverse(at).start()
     barrier = pltpu.get_barrier_semaphore()
     for step in range(1, n_row):
         other = lax.rem(row_at + step, n_row)
@@ -103,7 +109,7 @@
     pl.semaphore_wait(barrier, n_row + n_col - 2)
     each(n_row, lambda at: at == row_at, lambda at: col_copy(row_at, at).start())
     each(n_col, lambda at: at == col_at, lambda at: panel_copy(col_at, at).start())
-    for at in range(pieces):
+    for at in range(pieces // 2):
         widen(at)
     each(n_row, lambda at: at == row_at, lambda at: col_copy(at, at).wait_recv())
     keep = pltpu.make_async_copy(col_land, row_land.at[group], own_sem.at[0])
@@ -116,6 +122,10 @@
     col_scaled[...] = col_land[...] * halves
     col_move = pltpu.make_async_copy(col_scaled, col_ids, ids_sem.at[0])
     col_move.start()
+    for at in range(pieces):
+        load_inverse(at).start()
+    for at in range(pieces // 2, pieces):
+        widen(at)
     each(n_col, lambda at: at == col_at, lambda at: panel_copy(at, at).wait_recv())
     panel_scaled[...] = panel_land[...] * halves
     panel_move = pltpu.make_async_copy(panel_scaled, panel_ids, ids_sem.at[1])
@@ -137,6 +147,10 @@
         if block:
             narrow(picked, emb_ref, (block - 1) * width, width, (block - 1) * width)
     narrow(picked, emb_ref, (n_col - 1) * width, width, (n_col - 1) * width)
+    eye = lax.broadcasted_iota(jnp.int32, (LANES, LANES), 0) == lax.broadcasted_iota(jnp.int32, (LANES, LANES), 1)
+    for at in range(0, emb_ref.shape[0], LANES):
+        norm = jnp.broadcast_to(row_norm(emb_ref[at : at + LANES, :]), (LANES, LANES))
+        norm_ref[0:1, at : at + LANES] = jnp.sum(jnp.where(eye, norm, 0.0), axis=0, keepdims=True)
 
     @pl.when(forwards)
     def _():
@@ -184,9 +198,10 @@
             jax.ShapeDtypeStruct((teacher.shape[0] * halves, LANES), jnp.float32),
             jax.ShapeDtypeStruct(row_shape, jnp.int32),
             jax.ShapeDtypeStruct(inverse.shape, inverse.dtype),
+            jax.ShapeDtypeStruct((8, total), jnp.float32),
         ),
         in_specs=[hbm] * 4,
-        out_specs=(vmem,) * 4,
+        out_specs=(vmem,) * 5,
         scratch_shapes=[
             pltpu.VMEM(panel_shape, jnp.int32),
             pltpu.VMEM(col_shape, jnp.int32),
@@ -217,8 +232,8 @@
 
 
 def gram_kernel(
-    n_row, n_col, stretch, emb_ref, rows_in, table_ref, inv_ref, trail_hbm, own_hbm,
-    row_ids, picked, left_ref, cross_ref, fac_ref, back_ref, norm_ref, trail_ref,
+    n_row, n_col, stretch, emb_ref, rows_in, table_ref, inv_ref, norm_ref, trail_hbm, own_hbm,
+    row_ids, picked, left_ref, cross_ref, fac_ref, back_ref, trail_ref,
     ids_sem, own_sem, trail_sem,
 ):
     width = inv_ref.shape[0]
@@ -229,7 +244,7 @@
     n_rows = n_col * stretch
     n_cols = n_row * stretch
     groups = n_col // n_row
-    unit = 2.0 / embed * 1.4426950408889634
+    unit = unit_of(embed)
     row_at = lax.axis_index("row")
     col_at = lax.axis_index("col")
     tile = 512
@@ -238,15 +253,6 @@
 
     ids_move = pltpu.make_async_copy(rows_in, row_ids, ids_sem)
     ids_move.start()
-    eye = lax.broadcasted_iota(jnp.int32, (LANES, LANES), 0) == lax.broadcasted_iota(jnp.int32, (LANES, LANES), 1)
-
-    def down(value):
-        return jnp.sum(jnp.square(value.astype(jnp.float32)), axis=-1, keepdims=True) * unit
-
-    def across(start, count):
-        for at in range(start, start + count, LANES):
-            norm = jnp.broadcast_to(down(emb_ref[at : at + LANES, :]), (LANES, LANES))
-            norm_ref[0:1, at : at + LANES] = jnp.sum(jnp.where(eye, norm, 0.0), axis=0, keepdims=True)
 
     def inner(left, start, count):
         return nt_dot(left, emb_ref[start : start + count, :])
@@ -263,11 +269,11 @@
                 picked[(home + lane) * halves : (home + lane + 1) * halves, :] = row
             narrow(picked, left_ref, home, chunk, base)
 
-    picked_rows = 0
+    picked_rows, quiet = 0, blocks // 2
     hold = slice(tile, 2 * tile)
     for start in range(0, n_cols, tile):
         left = emb_ref[width + start : width + start + tile, :]
-        left_norm = down(left)
+        left_norm = row_norm(left)
         rows = slice(start, start + tile)
         product = inner(left, 0, block)
         for at in range(blocks + 1):
@@ -275,27 +281,24 @@
             held = product
             if at < blocks:
                 here = slice(at * block, (at + 1) * block)
-                if not start:
-                    across(at * block, block)
                 cross_ref[hold, here] = gaussian(held, left_norm, at * block, block).astype(jnp.bfloat16)
                 if at + 1 < blocks:
                     product = inner(left, (at + 1) * block, block)
             if at:
-                if at == 1 and not start:
-                    ids_move.wait()
                 fac_ref[rows, cols] = nt_dot(
                     cross_ref[hold, : at * block], inv_ref[cols, : at * block]
                 ).astype(jnp.bfloat16)
-                if not start:
-                    until = n_rows * at * (at + 1) // (blocks * (blocks + 1)) // chunk * chunk
+                if not start and at == quiet:
+                    ids_move.wait()
+                if not start and at >= quiet:
+                    until = n_rows * (at - quiet + 1) // (blocks - quiet + 1) // chunk * chunk
                     pick(picked_rows, until - picked_rows)
                     picked_rows = until
     own = pltpu.make_async_copy(
         fac_ref.at[pl.ds(pl.multiple_of(row_at * stretch, stretch), stretch), :], own_hbm, own_sem
     )
     own.start()
-    across(width, n_cols)
-    lefts = [(start, down(left_ref[start : start + tile, :])) for start in range(0, n_rows, tile)]
+    lefts = [(start, row_norm(left_ref[start : start + tile, :])) for start in range(0, n_rows, tile)]
 
     def cross_rows(tile_at, at):
         start, left_norm = lefts[tile_at]
@@ -365,7 +368,7 @@
     n_col = lax.axis_size("col")
     stretch = rest_ids.shape[2]
     width = inverse.shape[0]
-    emb, table, rows, inv = exchange(rest_ids, panel_ids, teacher, inverse, n_row, n_col)
+    emb, table, rows, inv, norms = exchange(rest_ids, panel_ids, teacher, inverse, n_row, n_col)
     n_rows = n_col * stretch
     n_cols = n_row * stretch
     embed = teacher.shape[1]
@@ -381,7 +384,7 @@
             jax.ShapeDtypeStruct((n_rows * n_row, stretch), jnp.float32),
             jax.ShapeDtypeStruct((stretch, width), jnp.bfloat16),
         ),
-        in_specs=[vmem] * 4,
+        in_specs=[vmem] * 5,
         out_specs=(hbm, hbm),
         scratch_shapes=[
             pltpu.SMEM(rows.shape, jnp.int32),
@@ -390,13 +393,12 @@
             pltpu.VMEM((2 * 512, width), jnp.bfloat16),
             pltpu.VMEM((n_cols, width), jnp.bfloat16),
             pltpu.VMEM((n_cols, width), jnp.bfloat16),
-            pltpu.VMEM((8, width + n_cols), jnp.float32),
             pltpu.VMEM((2 * 512 * n_row, stretch), jnp.float32),
             dma(()), dma(()), dma((2,)),
         ],
         compiler_params=pltpu.CompilerParams(vmem_limit_bytes=max(limit, held)),
         name="gram",
-    )(emb, rows, table, inv)
+    )(emb, rows, table, inv, norms)
     return (
         trailing.reshape(n_col, 1, stretch, n_row, 1, stretch),
         own_factor.reshape(1, 1, stretch, width),

time: 26.4 us -> 25.4 us (0.962)
  Pallas kernels: 25.7 us -> 24.6 us
    pallas_call x1, Pallas kernels: 14.3 us -> 13.3 us  [exchange(): pl.pallas_call(functools.partial(exchange_kernel, n_row, n_col), out_shap...]
where the time goes in v3:
time: 25.4 us; the launch traced here: 25.3 us
  Pallas kernels  24.6 us (97%)
  between operations  0.64 us (3%)
    pallas_call x1, Pallas kernels, exchange(): pl.pallas_call(functools.partial(exchange_kernel, n_row, n_col), out_shap...  13.3 us
    pallas_call x1, Pallas kernels, shards(): pl.pallas_call(functools.partial(gram_kernel, n_row, n_col, stretch), out...  11.3 us

profile of v3, /device:TPU:0, one launch (start us, length us, event | category | flops | bytes accessed | tf_op | source)
XLA Modules:
  0.0 25.3 jit_solution(6782554885162881508)
XLA Ops:
  0.6 13.3 %exchange.1 = (bf16[2560,256]{1,0:T(8,128)(2,1)S(1)}, f32[32768,128]{1,0:T(8,128)S(1)}, s32[2,4,1,128]{3,2,1,0:T(1,128)S(1)}, bf16[2048,2048]{1,0:T(8,128)(2,1)S(1)}, f32[8,2560]{1,0:T(8,128)S(1)}) custom-call(s32[1,1,128]{2,1,0:T(1,128)} %rest_hbm.1, s32[1,1,256]{2,1,0:T(1,128)} %bitcast.5, bf16[16384,256]{1,0:T(8,128)(2,1)} %table_hbm.1, ...), custom_call_target="tpu_custom_call" | custom-call | tf_op jit(solution)/shard_map/exchange/pallas_call | solution.py:194
  14.0 11.3 %gram.1 = (f32[4096,128]{1,0:T(8,128)}, bf16[128,2048]{1,0:T(8,128)(2,1)}) custom-call(bf16[2560,256]{1,0:T(8,128)(2,1)S(1)} %get-tuple-element.9.emb_ref, s32[2,4,1,128]{3,2,1,0:T(1,128)S(1)} %get-tuple-element.10.rows_in, f32[32768,128]{1,0:T(8,128)S(1)} %get-tuple-element.11.table_ref, bf16[2048,2048]{1,0:T(8,128)(2,1)S(1)} %get-tuple-element.12.inv_ref, ...), custom_call_target="tpu_custom_call" | custom-call | tf_op jit(solution)/shard_map/gram/pallas_call | solution.py:381

commit v4 on v3

--- a/solution.py
+++ b/solution.py
@@ -28,8 +28,12 @@
     return jnp.sum(jnp.square(value.astype(jnp.float32)), axis=-1, keepdims=True) * unit_of(value.shape[1])
 
 
+def gaussian(product, left_norm, right_norm, embed):
+    return jnp.exp2(product * (2.0 * unit_of(embed)) - (left_norm + right_norm))
+
+
 def exchange_kernel(
-    n_row, n_col, rest_hbm, panel_hbm, table_hbm, inv_hbm, emb_ref, table_ref, rows_out, inv_ref, norm_ref,
+    n_row, n_col, early, rest_hbm, panel_hbm, table_hbm, inv_hbm, emb_ref, table_ref, rows_out, inv_ref, norm_ref, cols_ref,
     panel_land, col_land, row_land, panel_scaled, col_scaled, panel_ids, col_ids, landed, picked,
     panel_send, row_send, col_send, panel_sem, row_sem, col_sem, table_sem, inv_sem, own_sem, ids_sem,
 ):
@@ -152,6 +156,15 @@
         norm = jnp.broadcast_to(row_norm(emb_ref[at : at + LANES, :]), (LANES, LANES))
         norm_ref[0:1, at : at + LANES] = jnp.sum(jnp.where(eye, norm, 0.0), axis=0, keepdims=True)
 
+    if early:
+        embed = emb_ref.shape[1]
+        left = emb_ref[first_col : first_col + n_row * stretch, :]
+        left_norm = row_norm(left)
+        for at in range(0, first_col, 256):
+            cols = slice(at, at + 256)
+            value = gaussian(nt_dot(left, emb_ref[cols, :]), left_norm, norm_ref[0:1, cols], embed)
+            cols_ref[:, cols] = value.astype(jnp.bfloat16)
+
     @pl.when(forwards)
     def _():
         keep.wait()
@@ -174,8 +187,14 @@
         each(n_col, lambda at: at == col_at, lambda at: row_copy(group, at).wait_send())
 
 
+def is_early(n_cols):
+    return n_cols == 512
+
+
 def own_limit(teacher, inverse, total):
-    return VMEM_BYTES - 4 * teacher.size - 2 * inverse.size - 2 * total * teacher.shape[1] - 12 * 1024 * 1024
+    n_cols = total - inverse.shape[0]
+    early = 2 * n_cols * inverse.shape[0] if is_early(n_cols) else 0
+    return VMEM_BYTES - 4 * teacher.size - 2 * inverse.size - 2 * total * teacher.shape[1] - early - 12 * 1024 * 1024
 
 
 def exchange(rest_ids, panel_ids, teacher, inverse, n_row, n_col):
@@ -190,18 +209,20 @@
     vmem = pl.BlockSpec(memory_space=pltpu.VMEM)
     hbm = pl.BlockSpec(memory_space=pltpu.HBM)
     dma = pltpu.SemaphoreType.DMA
+    early = is_early(n_row * stretch)
     operands = (rest_ids, panel_ids.reshape(1, 1, width), teacher, inverse)
     return pl.pallas_call(
-        functools.partial(exchange_kernel, n_row, n_col),
+        functools.partial(exchange_kernel, n_row, n_col, early),
         out_shape=(
             jax.ShapeDtypeStruct((total, teacher.shape[1]), teacher.dtype),
             jax.ShapeDtypeStruct((teacher.shape[0] * halves, LANES), jnp.float32),
             jax.ShapeDtypeStruct(row_shape, jnp.int32),
             jax.ShapeDtypeStruct(inverse.shape, inverse.dtype),
             jax.ShapeDtypeStruct((8, total), jnp.float32),
+            jax.ShapeDtypeStruct((n_row * stretch if early else 16, inverse.shape[0]), teacher.dtype),
         ),
         in_specs=[hbm] * 4,
-        out_specs=(vmem,) * 5,
+        out_specs=(vmem,) * 6,
         scratch_shapes=[
             pltpu.VMEM(panel_shape, jnp.int32),
             pltpu.VMEM(col_shape, jnp.int32),
@@ -232,7 +253,7 @@
 
 
 def gram_kernel(
-    n_row, n_col, stretch, emb_ref, rows_in, table_ref, inv_ref, norm_ref, trail_hbm, own_hbm,
+    n_row, n_col, stretch, emb_ref, rows_in, table_ref, inv_ref, norm_ref, cols_ref, trail_hbm, own_hbm,
     row_ids, picked, left_ref, cross_ref, fac_ref, back_ref, trail_ref,
     ids_sem, own_sem, trail_sem,
 ):
@@ -244,7 +265,6 @@
     n_rows = n_col * stretch
     n_cols = n_row * stretch
     groups = n_col // n_row
-    unit = unit_of(embed)
     row_at = lax.axis_index("row")
     col_at = lax.axis_index("col")
     tile = 512
@@ -257,8 +277,8 @@
     def inner(left, start, count):
         return nt_dot(left, emb_ref[start : start + count, :])
 
-    def gaussian(product, left_norm, start, count):
-        return jnp.exp2(product * (2.0 * unit) - (left_norm + norm_ref[0:1, start : start + count]))
+    def gauss(left, left_norm, start, count):
+        return gaussian(inner(left, start, count), left_norm, norm_ref[0:1, start : start + count], embed)
 
     def pick(start, count):
         for base in range(start, start + count, chunk):
@@ -270,23 +290,22 @@
             narrow(picked, left_ref, home, chunk, base)
 
     picked_rows, quiet = 0, blocks // 2
-    hold = slice(tile, 2 * tile)
+    early = is_early(n_cols)
+    hold = slice(0, tile) if early else slice(tile, 2 * tile)
+    crosses = cols_ref if early else cross_ref
     for start in range(0, n_cols, tile):
-        left = emb_ref[width + start : width + start + tile, :]
-        left_norm = row_norm(left)
         rows = slice(start, start + tile)
-        product = inner(left, 0, block)
+        if not early:
+            left = emb_ref[width + start : width + start + tile, :]
+            left_norm = row_norm(left)
         for at in range(blocks + 1):
             cols = slice((at - 1) * block, at * block)
-            held = product
-            if at < blocks:
-                here = slice(at * block, (at + 1) * block)
-                cross_ref[hold, here] = gaussian(held, left_norm, at * block, block).astype(jnp.bfloat16)
-                if at + 1 < blocks:
-                    product = inner(left, (at + 1) * block, block)
+            if at < blocks and not early:
+                value = gauss(left, left_norm, at * block, block)
+                cross_ref[hold, at * block : (at + 1) * block] = value.astype(jnp.bfloat16)
             if at:
                 fac_ref[rows, cols] = nt_dot(
-                    cross_ref[hold, : at * block], inv_ref[cols, : at * block]
+                    crosses[hold, : at * block], inv_ref[cols, : at * block]
                 ).astype(jnp.bfloat16)
                 if not start and at == quiet:
                     ids_move.wait()
@@ -302,8 +321,7 @@
 
     def cross_rows(tile_at, at):
         start, left_norm = lefts[tile_at]
-        product = inner(left_ref[start : start + tile, :], at * block, block)
-        value = gaussian(product, left_norm, at * block, block)
+        value = gauss(left_ref[start : start + tile, :], left_norm, at * block, block)
         home = tile_at % 2 * tile
         cross_ref[home : home + tile, at * block : (at + 1) * block] = value.astype(jnp.bfloat16)
 
@@ -339,7 +357,7 @@
             if last * n_row + n_row - 1 >= low * n_col:
                 span = slice(low * stretch, (low + pair) * stretch)
                 first = width + low * stretch
-                value = gaussian(inner(left, first, pair * stretch), left_norm, first, pair * stretch) - nt_dot(
+                value = gauss(left, left_norm, first, pair * stretch) - nt_dot(
                     cross_ref[home : home + tile, :], back_ref[span, :]
                 )
             else:
@@ -368,7 +386,7 @@
     n_col = lax.axis_size("col")
     stretch = rest_ids.shape[2]
     width = inverse.shape[0]
-    emb, table, rows, inv, norms = exchange(rest_ids, panel_ids, teacher, inverse, n_row, n_col)
+    emb, table, rows, inv, norms, crosses = exchange(rest_ids, panel_ids, teacher, inverse, n_row, n_col)
     n_rows = n_col * stretch
     n_cols = n_row * stretch
     embed = teacher.shape[1]
@@ -384,7 +402,7 @@
             jax.ShapeDtypeStruct((n_rows * n_row, stretch), jnp.float32),
             jax.ShapeDtypeStruct((stretch, width), jnp.bfloat16),
         ),
-        in_specs=[vmem] * 5,
+        in_specs=[vmem] * 6,
         out_specs=(hbm, hbm),
         scratch_shapes=[
             pltpu.SMEM(rows.shape, jnp.int32),
@@ -398,7 +416,7 @@
         ],
         compiler_params=pltpu.CompilerParams(vmem_limit_bytes=max(limit, held)),
         name="gram",
-    )(emb, rows, table, inv, norms)
+    )(emb, rows, table, inv, norms, crosses)
     return (
         trailing.reshape(n_col, 1, stretch, n_row, 1, stretch),
         own_factor.reshape(1, 1, stretch, width),

time: 25.4 us -> 25.7 us (1.012)
  Pallas kernels: 24.6 us -> 24.9 us
    pallas_call x1, Pallas kernels: 13.3 us -> 14.2 us  [exchange(): pl.pallas_call(functools.partial(exchange_kernel, n_row, n_col, early), o...]
    pallas_call x1, Pallas kernels: 11.3 us -> 10.6 us  [shards(): pl.pallas_call(functools.partial(gram_kernel, n_row, n_col, stretch), out...]
where the time goes in v4:
time: 25.7 us; the launch traced here: 25.5 us
  Pallas kernels  24.9 us (97%)
  between operations  0.64 us (2%)
    pallas_call x1, Pallas kernels, exchange(): pl.pallas_call(functools.partial(exchange_kernel, n_row, n_col, early), o...  14.2 us
    pallas_call x1, Pallas kernels, shards(): pl.pallas_call(functools.partial(gram_kernel, n_row, n_col, stretch), out...  10.6 us

profile of v4, /device:TPU:0, one launch (start us, length us, event | category | flops | bytes accessed | tf_op | source)
XLA Modules:
  0.0 25.5 jit_solution(5719972717933434728)
XLA Ops:
  0.6 14.2 %exchange.1 = (bf16[2560,256]{1,0:T(8,128)(2,1)S(1)}, f32[32768,128]{1,0:T(8,128)S(1)}, s32[2,4,1,128]{3,2,1,0:T(1,128)S(1)}, bf16[2048,2048]{1,0:T(8,128)(2,1)S...) custom-call(s32[1,1,128]{2,1,0:T(1,128)} %rest_hbm.1, s32[1,1,256]{2,1,0:T(1,128)} %bitcast.5, ...), custom_call_target="tpu_custom_call" | custom-call | tf_op jit(solution)/shard_map/exchange/pallas_call | solution.py:214
  14.9 10.6 %gram.1 = (f32[4096,128]{1,0:T(8,128)}, bf16[128,2048]{1,0:T(8,128)(2,1)}) custom-call(bf16[2560,256]{1,0:T(8,128)(2,1)S(1)} %get-tuple-element.10.emb_ref, s32[2,4,1,128]{3,2,1,0:T(1,128)S(1)} %get-tuple-element.11.rows_in, f32[32768,128]{1,0:T(8,128)S(1)} %get-tuple-element.12.table_ref, bf16[2048,2048]{1,0:T(8,128)(2,1)S(1)} %get-tuple-element.13.inv_ref, ...), custom_call_target="tpu_custom_call" | custom-call | tf_op jit(solution)/shard_map/gram/pallas_call | solution.py:399

commit v5 on v4

--- a/solution.py
+++ b/solution.py
@@ -294,7 +294,6 @@
     hold = slice(0, tile) if early else slice(tile, 2 * tile)
     crosses = cols_ref if early else cross_ref
     for start in range(0, n_cols, tile):
-        rows = slice(start, start + tile)
         if not early:
             left = emb_ref[width + start : width + start + tile, :]
             left_norm = row_norm(left)
@@ -304,9 +303,11 @@
                 value = gauss(left, left_norm, at * block, block)
                 cross_ref[hold, at * block : (at + 1) * block] = value.astype(jnp.bfloat16)
             if at:
-                fac_ref[rows, cols] = nt_dot(
-                    crosses[hold, : at * block], inv_ref[cols, : at * block]
-                ).astype(jnp.bfloat16)
+                for part in (0, tile // 2):
+                    fac_ref[start + part : start + part + tile // 2, cols] = nt_dot(
+                        crosses[hold.start + part : hold.start + part + tile // 2, : at * block],
+                        inv_ref[cols, : at * block],
+                    ).astype(jnp.bfloat16)
                 if not start and at == quiet:
                     ids_move.wait()
                 if not start and at >= quiet:
@@ -357,9 +358,12 @@
             if last * n_row + n_row - 1 >= low * n_col:
                 span = slice(low * stretch, (low + pair) * stretch)
                 first = width + low * stretch
-                value = gauss(left, left_norm, first, pair * stretch) - nt_dot(
-                    cross_ref[home : home + tile, :], back_ref[span, :]
-                )
+                half = tile // 2
+                value = [
+                    gauss(left[part : part + half], left_norm[part : part + half], first, pair * stretch)
+                    - nt_dot(cross_ref[home + part : home + part + half, :], back_ref[span, :])
+                    for part in (0, half)
+                ]
             else:
                 value = None
             for q in range(start // stretch, last + 1):
@@ -370,7 +374,7 @@
                         trail_ref[place, :] = jnp.zeros((stretch, stretch), jnp.float32)
                         continue
                     side = (p - low) * stretch
-                    part = value[top : top + stretch, side : side + stretch]
+                    part = value[top // half][top % half : top % half + stretch, side : side + stretch]
                     if q * n_row < p * n_col + n_col:
                         gap = (p * n_col + col_at - q * n_row - row_at) * stretch
                         part = jnp.where(ahead >= gap, part, 0.0)

time: 25.7 us -> 25.3 us (0.984)
  Pallas kernels: 24.9 us -> 24.5 us
    pallas_call x1, Pallas kernels: 10.6 us -> 10.3 us  [shards(): pl.pallas_call(functools.partial(gram_kernel, n_row, n_col, stretch), out...]
where the time goes in v5:
time: 25.3 us; the launch traced here: 25.2 us
  Pallas kernels  24.5 us (97%)
  between operations  0.64 us (3%)
    pallas_call x1, Pallas kernels, exchange(): pl.pallas_call(functools.partial(exchange_kernel, n_row, n_col, early), o...  14.2 us
    pallas_call x1, Pallas kernels, shards(): pl.pallas_call(functools.partial(gram_kernel, n_row, n_col, stretch), out...  10.3 us

profile of v5, /device:TPU:0, one launch (start us, length us, event | category | flops | bytes accessed | tf_op | source)
XLA Modules:
  0.0 25.2 jit_solution(9503266426335138563)
XLA Ops:
  0.6 14.2 %exchange.1 = (bf16[2560,256]{1,0:T(8,128)(2,1)S(1)}, f32[32768,128]{1,0:T(8,128)S(1)}, s32[2,4,1,128]{3,2,1,0:T(1,128)S(1)}, bf16[2048,2048]{1,0:T(8,128)(2,1)S...) custom-call(s32[1,1,128]{2,1,0:T(1,128)} %rest_hbm.1, s32[1,1,256]{2,1,0:T(1,128)} %bitcast.5, ...), custom_call_target="tpu_custom_call" | custom-call | tf_op jit(solution)/shard_map/exchange/pallas_call | solution.py:214
  14.9 10.3 %gram.1 = (f32[4096,128]{1,0:T(8,128)}, bf16[128,2048]{1,0:T(8,128)(2,1)}) custom-call(bf16[2560,256]{1,0:T(8,128)(2,1)S(1)} %get-tuple-element.10.emb_ref, s32[2,4,1,128]{3,2,1,0:T(1,128)S(1)} %get-tuple-element.11.rows_in, f32[32768,128]{1,0:T(8,128)S(1)} %get-tuple-element.12.table_ref, bf16[2048,2048]{1,0:T(8,128)(2,1)S(1)} %get-tuple-element.13.inv_ref, ...), custom_call_target="tpu_custom_call" | custom-call | tf_op jit(solution)/shard_map/gram/pallas_call | solution.py:403
